TPU v7x, 32 devices: a whole 2x2x4 slice. The times are simulated.
32 devices in a mesh: replica: 2 (over y), section: 2 (over core), seq: 8 (over z, x).
Axes of the slice: x: 2, y: 2, z: 4, core: 2. Of those that a mesh axis runs over, the one named last changes fastest.
Arguments:
- latents: float32 [2, 1024, 64], P('section', ('replica', 'seq')), parts along dimension 1, may hold values from -6 to 6
- cond: bfloat16 [2, 3, 1024, 4096], P('section', None, ('replica', 'seq')), parts along dimension 2, may hold values from -60 to 60
- embed: bfloat16 [2, 3, 64, 4096], P('section'), may hold values from -0.75 to 0.75
- audio_table: bfloat16 [2, 64, 4096], P('section', 'replica'), parts along dimension 1, may hold values from -6 to 6
- audio_map: int32 [64], P(('replica', 'seq')), parts along dimension 0, may hold values from 0 to 31
- out_proj: bfloat16 [2, 4096, 64], P('section'), may hold values from -0.5 to 0.5
- tile_start: int32 [16], P('replica'), parts along dimension 0, may hold values 0 or 1
- conv_input: bfloat16 [3, 3, 16, 512], P(None, None, None, 'section'), may hold values from -0.5 to 0.5
- conv_first: bfloat16 [3, 3, 512, 512], P(None, None, None, 'section'), may hold values from -0.09375 to 0.09375
- conv_second_up: bfloat16 [3, 3, 512, 256], P(None, None, None, 'section'), may hold values from -0.09375 to 0.09375
- conv_second: bfloat16 [3, 3, 256, 256], P(None, None, None, 'section'), may hold values from -0.125 to 0.125
- conv_third_up: bfloat16 [3, 3, 256, 128], P(None, None, None, 'section'), may hold values from -0.125 to 0.125
- conv_third: bfloat16 [3, 3, 128, 128], P(None, None, None, 'section'), may hold values from -0.1875 to 0.1875
- conv_color: bfloat16 [3, 3, 128, 3], replicated, may hold values from -0.1875 to 0.1875
- gain_first: float32 [512], replicated, may hold values from 0.1 to 1.9
- gain_second: float32 [256], replicated, may hold values from 0.1 to 1.9
- gain_third: float32 [128], replicated, may hold values from 0.1 to 1.9
- gain_color: float32 [128], replicated, may hold values from 0.1 to 1.9
Outputs:
- handoff: float32 [2, 1024, 64], P('section', ('replica', 'seq')), parts along dimension 1
- image: float32 [3, 128, 512], P(None, ('replica', 'seq')), parts along dimension 1
There are 2 independent parts, one for each index of `replica`. A program takes and returns all parts, laid end to end along the dimension named above; an argument that names none is the same for every part. Nothing has to cross between parts.
Inputs may be any that keep to these rules, and one draw needn't show every extreme that they name: `tile_start`: entry i is 1 where a decoder row tile begins at row block i; entry 0 is not read.
All inputs are finite; a program needn't handle non-finite values.
Results may differ from a plain program's by a relative error of at most 0.017.
Values may be sent and summed in bfloat16 or wider, within the bound.
A program may use at most 128 MiB of HBM per device.

v0:
```python
import math

import jax
import jax.numpy as jnp
from jax import lax
from jax.experimental import pallas as pl
from jax.experimental.pallas import tpu as pltpu
from jax.sharding import PartitionSpec as P

HEADS = 32
HSIZE = 128


step_size = -0.5
norm_eps = 1e-06


def full_weight(half):
    size = lax.axis_size("section")
    other = lax.ppermute(half, "section", [(i, (i + 1) % size) for i in range(size)])
    first = lax.axis_index("section") == 0
    return jnp.concatenate(
        [jnp.where(first, half, other), jnp.where(first, other, half)], axis=3
    )


def token_weight(weight):
    padded = jnp.pad(weight, ((2, 2), (2, 2), (0, 0), (0, 0)))
    cells = [[padded[1 - a : 7 - a, 1 - b : 7 - b] for b in (0, 1)] for a in (0, 1)]
    chans, outs = weight.shape[2:]
    stack = jnp.stack([jnp.stack(row) for row in cells])
    stack = stack.reshape(2, 2, 3, 2, 3, 2, chans, outs)
    return stack.transpose(2, 4, 3, 5, 6, 0, 1, 7).reshape(36 * chans, 4 * outs)


def lifted_weight(weight):
    wide = weight.astype(jnp.float32)
    taps = lambda w, axis: [
        [lax.index_in_dim(w, 0, axis, False),
         lax.index_in_dim(w, 1, axis, False) + lax.index_in_dim(w, 2, axis, False)],
        [lax.index_in_dim(w, 0, axis, False) + lax.index_in_dim(w, 1, axis, False),
         lax.index_in_dim(w, 2, axis, False)],
    ]
    rows = taps(wide, 0)
    cells = []
    for a in (0, 1):
        for b in (0, 1):
            parts = [taps(rows[a][p], 0)[b][q] for p in (0, 1) for q in (0, 1)]
            cells.append(jnp.concatenate(parts, axis=0).astype(jnp.bfloat16))
    return jnp.stack(cells)


def decode_kernel(
    keep, tokens, w_in, w_first, w_up2, w_second, w_up3, w_third, w_color,
    g1, g2, g3, g4, out, a1, p1, x1, a2, p2, x2, a3, p3, p4,
):
    cols = tokens.shape[1]
    f32, bf16 = jnp.float32, jnp.bfloat16
    k_a, k_b, k_c, k_d = keep[0], keep[1], keep[2], keep[3]

    def moved(value, by):
        position = lax.broadcasted_iota(jnp.int32, value.shape, 0)
        if by > 0:
            return jnp.where(position > 0, pltpu.roll(value, 1, 0), 0.0)
        return jnp.where(position < cols - 1, pltpu.roll(value, cols - 1, 0), 0.0)

    def put(buf, index, value):
        phases = value.shape[0]
        buf[index, 1 : phases + 1] = value.astype(bf16)
        buf[index, 0] = moved(value[phases - 1], 1).astype(bf16)
        buf[index, phases + 1] = moved(value[0], -1).astype(bf16)

    def act(value, gain):
        square = jnp.mean(value * value, axis=-1, keepdims=True)
        scaled = value * lax.rsqrt(square + norm_eps) * gain[...]
        return jax.nn.silu(scaled)

    def fill(source, buf, count, where_to, masked, gain=None, offset=0):
        @pl.loop(0, count)
        def _(i):
            value = source[i + offset].astype(f32)
            put(buf, where_to(i), value if gain is None else act(value, gain))

        for target, origin, factor in masked:
            if origin is None:
                buf[target] = jnp.zeros(buf.shape[1:], bf16)
            else:
                buf[target] = (buf[origin].astype(f32) * factor).astype(bf16)

    def spots(*bounds):
        def start(o):
            index = o
            for bound in bounds:
                index = index + 2 * (o >= bound).astype(jnp.int32)
            return index

        return start

    def window(buf, start, rows, taps_r, taps_c, phases):
        parts = []
        for p in taps_r:
            for q in taps_c:
                block = buf[pl.ds(start + p, rows), q : q + phases]
                parts.append(block.reshape(rows * phases * cols, block.shape[-1]))
        return jnp.concatenate(parts, axis=1)

    def dot(x, w):
        return jnp.dot(x, w, preferred_element_type=f32)

    full = tokens[...].astype(f32)
    count = full.shape[0]
    zero = jnp.zeros((1,) + full.shape[1:], f32)
    ks = (k_a, k_b, k_c, k_d)
    above = jnp.concatenate([zero] + [full[i : i + 1] * ks[i] for i in range(count - 1)])
    below = jnp.concatenate([full[i + 1 : i + 2] * ks[i] for i in range(count - 1)] + [zero])
    pieces = []
    for rows in (above, full, below):
        left = jnp.stack([moved(rows[i], 1) for i in range(count)])
        right = jnp.stack([moved(rows[i], -1) for i in range(count)])
        pieces += [left, rows, right]
    x = jnp.concatenate(pieces, axis=2).astype(bf16).reshape(count * cols, -1)
    c1 = a1.shape[-1]
    for a in (0, 1):
        for b in (0, 1):
            j = 2 * a + b
            y = dot(x, w_in[:, j * c1 : (j + 1) * c1]).astype(bf16)
            for i in range(count):
                a1[2 * i + a, b] = y[i * cols : (i + 1) * cols]

    def spot1(i):
        return i + 1 + 2 * (i >= 2).astype(jnp.int32) + 2 * (i >= 4).astype(jnp.int32)

    inner = ((3, 5, k_b), (4, 2, k_b), (7, 9, k_c), (8, 6, k_c))
    fill(a1, p1, 6, spot1, inner, g1, 2)
    for target, origin, factor in ((0, 1, k_a), (11, 8, k_d)):
        put(p1, target, act(a1[origin].astype(f32), g1) * factor)

    @pl.loop(0, 3)
    def _(i):
        y = dot(window(p1, 4 * i, 2, (0, 1, 2), (0, 1, 2), 2), w_first[...])
        base = a1[pl.ds(2 * i + 2, 2)]
        a1[pl.ds(2 * i + 2, 2)] = (base.astype(f32) + y.reshape(base.shape)).astype(bf16)

    fill(a1, x1, 6, spot1, inner + ((0, None, 0), (11, None, 0)), None, 2)

    @pl.loop(0, 3)
    def _(i):
        for a in (0, 1):
            for b in (0, 1):
                y = dot(window(x1, 4 * i, 2, (a, a + 1), (b, b + 1), 2), w_up2[2 * a + b])
                y = y.astype(bf16).reshape(2, 2, cols, -1)
                for r in (0, 1):
                    for f in (0, 1):
                        a2[4 * i + 2 * r + a, 2 * f + b] = y[r, f]

    fill(
        a2, p2, 10,
        lambda i: i + 2 * (i >= 3).astype(jnp.int32) + 2 * (i >= 7).astype(jnp.int32),
        ((3, 5, k_b), (4, 2, k_b), (9, 11, k_c), (10, 8, k_c)), g2, 1,
    )
    start2 = spots(2, 6)

    @pl.loop(0, 8)
    def _(o):
        y = dot(window(p2, start2(o), 1, (0, 1, 2), (0, 1, 2), 4), w_second[...])
        base = a2[o + 2]
        a2[o + 2] = (base.astype(f32) + y.reshape(base.shape)).astype(bf16)

    fill(
        a2, x2, 8,
        lambda i: i + 2 * (i >= 2).astype(jnp.int32) + 2 * (i >= 6).astype(jnp.int32),
        ((2, 4, k_b), (3, 1, k_b), (8, 10, k_c), (9, 7, k_c)), None, 2,
    )
    start3 = spots(1, 5)

    @pl.loop(0, 6)
    def _(o):
        for a in (0, 1):
            for b in (0, 1):
                y = dot(window(x2, start3(o), 1, (a, a + 1), (b, b + 1), 4), w_up3[2 * a + b])
                y = y.astype(bf16).reshape(4, cols, -1)
                for f in range(4):
                    a3[2 * o + a, 2 * f + b] = y[f]

    fill(
        a3, p3, 12,
        lambda i: i + 2 * (i >= 2).astype(jnp.int32) + 2 * (i >= 10).astype(jnp.int32),
        ((2, 4, k_b), (3, 1, k_b), (12, 14, k_c), (13, 11, k_c)), g3,
    )
    start4 = spots(1, 9)

    @pl.loop(0, 10)
    def _(o):
        y = dot(window(p3, start4(o), 1, (0, 1, 2), (0, 1, 2), 8), w_third[...])
        base = a3[o + 1]
        value = (base.astype(f32) + y.reshape(base.shape)).astype(bf16).astype(f32)
        put(p4, o, act(value, g4))

    for target, factor in ((0, k_b), (9, k_c)):
        p4[target] = (p4[target].astype(f32) * factor).astype(bf16)

    @pl.loop(0, 8)
    def _(o):
        patch = window(p4, o, 1, (0, 1, 2), (0, 1, 2), 8)
        out[o] = lax.dot_general(
            w_color[...], patch, (((1,), (1,)), ((), ())), preferred_element_type=f32
        )


def decode(tokens, keep, weights, gains):
    count, cols = tokens.shape[:2]
    c1, c2, c3 = (w.shape[-1] for w in (weights[1], weights[3], weights[5]))
    bf16 = jnp.bfloat16
    vmem = pl.BlockSpec(memory_space=pltpu.VMEM)
    rgb = weights[6].shape[0]
    return pl.pallas_call(
        decode_kernel,
        out_shape=jax.ShapeDtypeStruct((8, rgb, 8 * cols), jnp.float32),
        in_specs=[pl.BlockSpec(memory_space=pltpu.SMEM)] + [vmem] * 12,
        out_specs=vmem,
        scratch_shapes=[
            pltpu.VMEM((2 * count, 2, cols, c1), bf16),
            pltpu.VMEM((12, 4, cols, c1), bf16),
            pltpu.VMEM((12, 4, cols, c1), bf16),
            pltpu.VMEM((12, 4, cols, c2), bf16),
            pltpu.VMEM((14, 6, cols, c2), bf16),
            pltpu.VMEM((12, 6, cols, c2), bf16),
            pltpu.VMEM((12, 8, cols, c3), bf16),
            pltpu.VMEM((16, 10, cols, c3), bf16),
            pltpu.VMEM((10, 10, cols, c3), bf16),
        ],
        compiler_params=pltpu.CompilerParams(vmem_limit_bytes=56 * 1024 * 1024),
    )(keep, tokens, *weights, *gains)


def attend(queries, key_rows, value_rows, heads_here):
    query_count = queries.shape[0]
    head_width = queries.shape[1]
    head_size = head_width // heads_here
    scale = 1.0 / math.sqrt(head_size)
    key_heads = key_rows.reshape(-1, heads_here, head_size)
    value_heads = value_rows.reshape(-1, heads_here, head_size)
    query_block = min(512, query_count)
    blocks = queries.reshape(query_count // query_block, query_block, heads_here, head_size)

    def one_block(block_rows):
        scores = (
            jnp.einsum("qhd,khd->hqk", block_rows, key_heads, preferred_element_type=jnp.float32)
            * scale
        )
        row_max = jnp.max(scores, axis=2, keepdims=True)
        weights = jnp.exp(scores - row_max)
        denominator = jnp.sum(weights, axis=2, keepdims=True)
        attended = (
            jnp.einsum(
                "hqk,khd->hqd",
                weights.astype(jnp.bfloat16),
                value_heads,
                preferred_element_type=jnp.float32,
            )
            / denominator
        )
        return jnp.transpose(attended, (1, 0, 2)).astype(jnp.bfloat16)

    return lax.map(one_block, blocks).reshape(query_count, head_width)


def spread_full(projected_all, splits, groups, head_width):
    tokens_here = projected_all.shape[1]
    half_rows = tokens_here // splits
    devices = groups * splits
    pair_rows = projected_all[1:].reshape(2, tokens_here, groups, 1, head_width)
    pair_rows = jnp.broadcast_to(pair_rows, (2, tokens_here, groups, splits, head_width)).reshape(
        2, tokens_here, devices, head_width
    )
    query_rows = (
        projected_all[0]
        .reshape(splits, half_rows, groups, head_width)
        .transpose(1, 2, 0, 3)
        .reshape(1, half_rows, devices, head_width)
    )
    got_pairs, got_queries = (
        lax.all_to_all(pair_rows, "seq", split_axis=2, concat_axis=1, tiled=True),
        lax.all_to_all(query_rows, "seq", split_axis=2, concat_axis=1, tiled=True),
    )
    return (
        got_queries.reshape(-1, head_width),
        got_pairs[0].reshape(-1, head_width),
        got_pairs[1].reshape(-1, head_width),
    )


def body(
    latents,
    cond,
    embed,
    audio_table,
    audio_map,
    out_proj,
    tile_start,
    conv_input,
    conv_first,
    conv_second_up,
    conv_second,
    conv_third_up,
    conv_third,
    conv_color,
    gain_first,
    gain_second,
    gain_third,
    gain_color,
):
    split_convs = (conv_input, conv_first, conv_second_up, conv_second, conv_third_up, conv_third)
    latent = latents[0]
    tokens_here = latent.shape[0]
    low = latent.astype(jnp.bfloat16)
    projected = jnp.einsum("tp,cph->cth", low, embed[0], preferred_element_type=jnp.float32)
    frame_count = audio_table.shape[1]
    picks = (audio_map[:, None] == lax.broadcasted_iota(jnp.int32, (1, frame_count), 1)).astype(
        jnp.bfloat16
    )
    per_frame = jnp.dot(picks, audio_table[0], preferred_element_type=jnp.float32)
    audio = jnp.repeat(per_frame, tokens_here // audio_map.shape[0], axis=0)
    projected_all = jnp.stack(
        [
            (projected[0] + cond[0, 0] + audio).astype(jnp.bfloat16),
            (projected[1] + cond[0, 1]).astype(jnp.bfloat16),
            (projected[2] + cond[0, 2] + audio).astype(jnp.bfloat16),
        ]
    )
    devices = lax.axis_size("seq")
    splits = max(devices // HEADS, 1)
    per_device = max(HEADS // devices, 1)
    groups = HEADS // per_device
    head_width = per_device * HSIZE
    queries, key_rows, value_rows = spread_full(projected_all, splits, groups, head_width)
    attended = attend(queries, key_rows, value_rows, per_device)
    position = lax.axis_index("seq")
    group_rows = lax.dynamic_slice_in_dim(
        out_proj[0], (position // splits) * head_width, head_width, 0
    )
    partial = jnp.dot(attended, group_rows, preferred_element_type=jnp.float32)
    half_rows = tokens_here // splits
    partial = partial.reshape(devices, 1, half_rows, -1)
    if splits > 1:
        mine = lax.broadcasted_iota(jnp.int32, (1, splits, 1, 1), 1) == position % splits
        partial = jnp.where(mine, partial, 0.0)
    partial = partial.reshape(devices, tokens_here, -1)
    parts = lax.all_to_all(partial, "seq", split_axis=0, concat_axis=0, tiled=True)
    outcome = latent + step_size * jnp.sum(parts, axis=0)
    size = lax.axis_size("section")
    handed = lax.ppermute(outcome, "section", [(i, (i + 1) % size) for i in range(size)])
    final = jnp.where(lax.axis_index("section") == size - 1, outcome, handed)
    low_final = final.astype(jnp.bfloat16)
    rows = []
    for by in (-2, -1, 0, 1, 2):
        if by == 0:
            rows.append(low_final)
        else:
            pairs = [(i, i - by) for i in range(devices) if 0 <= i - by < devices]
            rows.append(lax.ppermute(low_final, "seq", pairs))
    tokens = jnp.stack(rows)
    block = position + jnp.arange(-2, 2)
    following = jnp.clip(block + 1, 0, devices - 1)
    inside = jnp.logical_and(block >= 0, block + 1 < devices)
    keep = jnp.where(jnp.logical_and(inside, tile_start[following] == 0), 1.0, 0.0)
    flat = lambda w: w.reshape(-1, w.shape[-1])
    w_input, w_first, w_up2, w_second, w_up3, w_third = [full_weight(w) for w in split_convs]
    color = jnp.pad(flat(conv_color).T, ((0, 8 - conv_color.shape[3]), (0, 0)))
    weights = (
        token_weight(w_input), flat(w_first), lifted_weight(w_up2), flat(w_second),
        lifted_weight(w_up3), flat(w_third), color,
    )
    gains = tuple(g[None] for g in (gain_first, gain_second, gain_third, gain_color))
    colors = decode(tokens, keep.astype(jnp.float32), weights, gains)
    rgb = conv_color.shape[3]
    image = colors[:, :rgb].reshape(8, rgb, 8, -1).transpose(1, 0, 3, 2).reshape(rgb, 8, -1)
    return (handed[None], image)


def solution(mesh):
    in_specs = (
        P("section", ("replica", "seq"), None),
        P("section", None, ("replica", "seq"), None),
        P("section", None, None, None),
        P("section", "replica", None),
        P(("replica", "seq")),
        P("section", None, None),
        P("replica"),
        P(None, None, None, "section"),
        P(None, None, None, "section"),
        P(None, None, None, "section"),
        P(None, None, None, "section"),
        P(None, None, None, "section"),
        P(None, None, None, "section"),
        P(),
        P(),
        P(),
        P(),
        P(),
    )
    out_specs = (P("section", ("replica", "seq"), None), P(None, ("replica", "seq"), None))
    return jax.shard_map(body, mesh=mesh, in_specs=in_specs, out_specs=out_specs, check_vma=False)
```

profile of v0, /device:TPU:0, one launch (start us, length us, event | category | flops | bytes accessed | tf_op | source)
XLA Modules:
  0.0 170.9 jit_solution(314064391693432127)
XLA Ops:
  3.6 1.4 convolution_bitcast_fusion
  8.7 7.3 %all-to-all-start = ((bf16[1,64,8,512]{3,1,0,2:T(8,128)(2,1)}), bf16[1,64,8,512]{3,1,0,2:T(8,128)(2,1)S(1)}, u32[]{:S(2)}, u32[]{:S(2)}) async-start(bf16[1,64,8,512]{3,1,0,2:T(8,128)(2,1)} %copy.70), calls=%async_computation | async-start | bytes 1048576 | tf_op jit(solution)/shard_map/all_to_all | solution.py:284
  19.8 2.1 %pad_maximum_fusion.2 = bf16[2,64,8,512]{3,1,0,2:T(8,128)(2,1)} fusion(bf16[1,64,8,512]{3,1,0,2:T(8,128)(2,1)S(1)} %get-tuple-element.76, bf16[1,64,8,512]{3,1,0,2:T(8,128)(2,1)} %get-tuple-element.77), kind=kLoop, calls=%fused_computation.39 | loop fusion | flops 524288 | bytes 2097152 | tf_op jit(solution)/shard_map/stack | solution.py:324
  27.5 8.9 %maximum_bitcast_fusion = bf16[3,3,2,2,16,2,2,512]{7,6,5,4,3,2,1,0:T(2,128)(2,1)} fusion(bf16[1,1,3,2,3,2,16,512]{7,1,0,6,5,3,4,2:T(2,128)(2,1)S(1)} %copy.81, bf16[1,1,3,2,3,2,16,512]{7,1,0,6,5,3,4,2:T(2,128)(2,1)S(1)} %copy.80, bf16[1,1,3,2,3,2,16,512]{7,1,0,6,5,3,4,2:T(2,128)(2,1)S(1)} %copy.79, bf16[1,1,3,2,3,2,16,512]{7,1,0,6,5,3,4,2:T(2,128)(2,1)S(1)} %copy.78), kind=kLoop, calls=%fused_computation.12 | loop fusion | flops 9437184 | bytes 4718592 | tf_op jit(solution)/shard_map/transpose | solution.py:33
  36.5 6.6 %reshape.675.w_in = bf16[576,2048]{1,0:T(8,128)(2,1)} reshape(bf16[3,3,2,2,16,2,2,512]{7,6,5,4,3,2,1,0:T(2,128)(2,1)} %maximum_bitcast_fusion) | data formatting | bytes 4718592 | tf_op jit(solution)/shard_map/reshape | solution.py:33
  46.0 2.7 %maximum_maximum_fusion.1.w_up3 = bf16[4,1024,128]{2,1,0:T(8,128)(2,1)} fusion(bf16[1,256,128]{2,1,0:T(8,128)(2,1)S(1)} %get-tuple-element.44, bf16[1,256,128]{2,1,0:T(8,128)(2,1)S(1)} %get-tuple-element.47, bf16[1,256,128]{2,1,0:T(8,128)(2,1)S(1)} %get-tuple-element.82, bf16[1,256,128]{2,1,0:T(8,128)(2,1)S(1)} %get-tuple-element.84, ...), kind=kLoop, calls=%fused_computation.40 | loop fusion | flops 16777216 | bytes 2097152 | tf_op jit(solution)/shard_map/stack | solution.py:50
  48.6 5.9 %all-to-all-start.1 = ((bf16[2,64,8,512]{3,1,0,2:T(8,128)(2,1)}), bf16[2,64,8,512]{3,1,0,2:T(8,128)(2,1)S(1)}, u32[]{:S(2)}, u32[]{:S(2)}) async-start(bf16[2,64,8,512]{3,1,0,2:T(8,128)(2,1)} %pad_maximum_fusion.2), calls=%async_computation.1 | async-start | bytes 2097152 | tf_op jit(solution)/shard_map/all_to_all | solution.py:283
  54.6 1.4 broadcast_select_fusion.7
  57.3 1.4 broadcast_select_fusion.3
  59.6 1.7 copy-done.3
  63.2 17.3 %all-to-all-done.1 = bf16[2,64,8,512]{3,1,0,2:T(8,128)(2,1)S(1)} async-done(((bf16[2,64,8,512]{3,1,0,2:T(8,128)(2,1)}), bf16[2,64,8,512]{3,1,0,2:T(8,128)(2,1)S(1)}, u32[]{:S(2)}, u32[]{:S(2)}) %all-to-all-start.1) | async-done | bytes 1048608 | tf_op jit(solution)/shard_map/all_to_all | solution.py:283
  86.1 3.6 %all-to-all-start.2 = ((f32[8,1,4096]{2,1,0:T(1,128)}), f32[8,1,4096]{2,1,0:T(1,128)S(1)}, u32[]{:S(2)}, u32[]{:S(2)}) async-start(f32[8,1,4096]{2,1,0:T(1,128)} %reshape.719), calls=%async_computation.2 | async-start | bytes 262144 | tf_op jit(solution)/shard_map/all_to_all | solution.py:349
  89.8 2.5 %fusion.32 = (bf16[1,512,256]{2,1,0:T(8,128)(2,1)S(1)}, bf16[1,512,256]{2,1,0:T(8,128)(2,1)}, bf16[1,512,256]{2,1,0:T(8,128)(2,1)}, bf16[1,512,256]{2,1,0:T(8,128)(2,1)}) fusion(f32[3,3,512,256]{3,2,1,0:T(8,128)} %copy-done.3), kind=kLoop, calls=%fused_computation.77 | loop fusion | bytes 2097152 | tf_op jit(solution)/shard_map/concatenate | solution.py:49
  92.3 4.9 %all-to-all-done.2 = f32[8,1,4096]{2,1,0:T(1,128)S(1)} async-done(((f32[8,1,4096]{2,1,0:T(1,128)}), f32[8,1,4096]{2,1,0:T(1,128)S(1)}, u32[]{:S(2)}, u32[]{:S(2)}) %all-to-all-start.2) | async-done | bytes 131104 | tf_op jit(solution)/shard_map/all_to_all | solution.py:349
  98.9 2.2 %fusion.40 = (bf16[1,512,256]{2,1,0:T(8,128)(2,1)S(1)}, bf16[1,512,256]{2,1,0:T(8,128)(2,1)S(1)}, bf16[1,512,256]{2,1,0:T(8,128)(2,1)S(1)}, bf16[1,512,256]{2,1,0:T(8,128)(2,1)S(1)}) fusion(f32[3,3,512,256]{3,2,1,0:T(8,128)} %copy-done.3), kind=kLoop, calls=%fused_computation.85 | loop fusion | flops 1048576 | bytes 4194304 | tf_op jit(solution)/shard_map/concatenate | solution.py:49
  101.1 1.9 %collective-permute-start.1 = (bf16[64,64]{1,0:T(8,128)(2,1)S(1)}, bf16[64,64]{1,0:T(8,128)(2,1)S(1)}, u32[]{:S(2)}, u32[]{:S(2)}) collective-permute-start(bf16[64,64]{1,0:T(8,128)(2,1)S(1)} %select_convert_fusion), channel_id=1, source_target_pairs={{0,2},{1,3},{2,4},{3,5},{4,6},{5,7},{8,10},{9,11},{10,12},{11,13},... | collective-permute-start | bytes 24584 | tf_op jit(solution)/shard_map/ppermute | solution.py:361
  103.1 10.5 %maximum_maximum_fusion.w_up2 = bf16[4,2048,256]{2,1,0:T(8,128)(2,1)} fusion(bf16[1,512,256]{2,1,0:T(8,128)(2,1)S(1)} %copy-done.13, bf16[1,512,256]{2,1,0:T(8,128)(2,1)S(1)} %get-tuple-element.22, bf16[1,512,256]{2,1,0:T(8,128)(2,1)S(1)} %copy-done.10, bf16[1,512,256]{2,1,0:T(8,128)(2,1)S(1)} %get-tuple-element.80, ...), kind=kLoop, calls=%fused_computation.3 | loop fusion | flops 67108864 | bytes 8388608 | tf_op jit(solution)/shard_map/stack | solution.py:50
  113.6 3.2 %collective-permute-start.2 = (bf16[64,64]{1,0:T(8,128)(2,1)S(1)}, bf16[64,64]{1,0:T(8,128)(2,1)S(1)}, u32[]{:S(2)}, u32[]{:S(2)}) collective-permute-start(bf16[64,64]{1,0:T(8,128)(2,1)S(1)} %select_convert_fusion), channel_id=1, source_target_pairs={{0,1},{1,2},{2,3},{3,4},{4,5},{5,6},{6,7},{8,9},{9,10},{10,11},{11... | collective-permute-start | bytes 24584 | tf_op jit(solution)/shard_map/ppermute | solution.py:361
  118.1 1.6 collective-permute-start.4
  119.7 2.7 %collective-permute-done.3 = bf16[64,64]{1,0:T(8,128)(2,1)S(1)} collective-permute-done((bf16[64,64]{1,0:T(8,128)(2,1)S(1)}, bf16[64,64]{1,0:T(8,128)(2,1)S(1)}, u32[]{:S(2)}, u32[]{:S(2)}) %collective-permute-start.3) | collective-permute-done | bytes 8224 | tf_op jit(solution)/shard_map/ppermute | solution.py:361
  122.5 2.5 %collective-permute-done.4 = bf16[64,64]{1,0:T(8,128)(2,1)S(1)} collective-permute-done((bf16[64,64]{1,0:T(8,128)(2,1)S(1)}, bf16[64,64]{1,0:T(8,128)(2,1)S(1)}, u32[]{:S(2)}, u32[]{:S(2)}) %collective-permute-start.4) | collective-permute-done | bytes 8224 | tf_op jit(solution)/shard_map/ppermute | solution.py:361
  125.0 2.0 %broadcast_select_fusion.1 = (bf16[3,3,512,256]{3,2,1,0:T(8,128)(2,1)S(1)}, bf16[3,3,512,256]{3,2,1,0:T(8,128)(2,1)S(1)}) fusion(bf16[3,3,512,256]{3,2,1,0:T(8,128)(2,1)S(1)} %copy-done.4, bf16[3,3,512,256]{3,2,1,0:T(8,128)(2,1)} %collective-permute-done.6, pred[]{:T(512)S(6)} %eq.32), kind=kLoop, calls=%fused_computation.15 | loop fusion | flops 2359296 | bytes 9437185 | tf_op jit(solution)/shard_map/jit(_where)/select_n | solution.py:23
  127.0 2.6 %pad_maximum_fusion = bf16[3,3,512,512]{3,2,1,0:T(8,128)(2,1)} fusion(bf16[3,3,512,256]{3,2,1,0:T(8,128)(2,1)S(1)} %get-tuple-element.28, bf16[3,3,512,256]{3,2,1,0:T(8,128)(2,1)S(1)} %get-tuple-element.27), kind=kLoop, calls=%fused_computation.2 | loop fusion | flops 9437184 | bytes 9437184 | tf_op jit(solution)/shard_map/concatenate | solution.py:22
  129.5 38.4 %shard_map.185 = f32[8,8,512]{2,1,0:T(8,128)} custom-call(f32[4]{0:T(128)} %and_select_fusion.keep, bf16[5,64,64]{2,1,0:T(8,128)(2,1)} %copy-done.18, bf16[576,2048]{1,0:T(8,128)(2,1)} %reshape.675.w_in, bf16[4608,512]{1,0:T(8,128)(2,1)} %bitcast.179, bf16[4,2048,256]{2,1,0:T(8,128)(2,1)} %maximum_maximum_fusion.w_up2, bf16[2304,256]{1,0:T(8,128)(2,1)} %bitcast.182, ...), custom_call_target="tpu_custom_call" | custom-call | tf_op jit(solution)/shard_map/pallas_call | solution.py:216
  (126 shorter events, 34.2 us)
Async XLA Ops:
  0.6 43.4 %collective-permute-start.9 = (bf16[3,3,256,64]{2,3,1,0:T(8,128)(2,1)}, bf16[3,3,256,64]{2,3,1,0:T(8,128)(2,1)}, u32[]{:S(2)}, u32[]{:S(2)}) collective-permute-start(bf16[3,3,256,64]{2,3,1,0:T(8,128)(2,1)} %param.29), channel_id=1, source_target_pairs={{0,8},{8,0},{1,9},{9,1},{2,10},{10,2},{3,11},{11,3},{4,12},{12,4},... | collective-permute-start | bytes 884744 | tf_op jit(solution)/shard_map/ppermute | solution.py:20
  1.2 56.1 %collective-permute-start.7 = (bf16[3,3,512,128]{3,2,1,0:T(8,128)(2,1)}, bf16[3,3,512,128]{3,2,1,0:T(8,128)(2,1)}, u32[]{:S(2)}, u32[]{:S(2)}) collective-permute-start(bf16[3,3,512,128]{3,2,1,0:T(8,128)(2,1)} %param.27), channel_id=1, source_target_pairs={{0,8},{8,0},{1,9},{9,1},{2,10},{10,2},{3,11},{11,3},{4,12},{12,4},... | collective-permute-start | bytes 3538952 | tf_op jit(solution)/shard_map/ppermute | solution.py:20
  7.3 8.7 %copy-start.19 = (bf16[3,3,16,256]{3,2,1,0:T(8,128)(2,1)S(1)}, bf16[3,3,16,256]{3,2,1,0:T(8,128)(2,1)}, u32[]{:S(2)}) copy-start(bf16[3,3,16,256]{3,2,1,0:T(8,128)(2,1)} %param.25) | copy-start | bytes 221188
  7.3 9.4 %copy-start.15 = (bf16[3,3,256,64]{2,3,1,0:T(8,128)(2,1)S(1)}, bf16[3,3,256,64]{2,3,1,0:T(8,128)(2,1)}, u32[]{:S(2)}) copy-start(bf16[3,3,256,64]{2,3,1,0:T(8,128)(2,1)} %param.29) | copy-start | bytes 884740
  7.7 9.3 %copy-start.2 = (s32[8]{0:T(128)S(1)}, s32[8]{0:T(128)}, u32[]{:S(2)}) copy-start(s32[8]{0:T(128)} %param.24) | copy-start | bytes 100
  8.7 10.5 %copy-start.20 = (bf16[3,3,128,3]{2,3,1,0:T(4,128)(2,1)S(1)}, bf16[3,3,128,3]{2,3,1,0:T(4,128)(2,1)}, u32[]{:S(2)}) copy-start(bf16[3,3,128,3]{2,3,1,0:T(4,128)(2,1)} %param.31) | copy-start | bytes 20740
  8.7 39.9 %all-to-all-start = ((bf16[1,64,8,512]{3,1,0,2:T(8,128)(2,1)}), bf16[1,64,8,512]{3,1,0,2:T(8,128)(2,1)S(1)}, u32[]{:S(2)}, u32[]{:S(2)}) async-start(bf16[1,64,8,512]{3,1,0,2:T(8,128)(2,1)} %copy.70), calls=%async_computation | async-start | bytes 1048576 | tf_op jit(solution)/shard_map/all_to_all | solution.py:284
  16.1 5.9 %collective-permute-start.5 = (bf16[3,3,16,256]{3,2,1,0:T(8,128)(2,1)S(1)}, bf16[3,3,16,256]{3,2,1,0:T(8,128)(2,1)S(1)}, u32[]{:S(2)}, u32[]{:S(2)}) collective-permute-start(bf16[3,3,16,256]{3,2,1,0:T(8,128)(2,1)S(1)} %copy-done.19), channel_id=1, source_target_pairs={{0,8},{8,0},{1,9},{9,1},{2,10},{10,2},{3,11},{11,3},{4,12},{12,4},... | collective-permute-start | bytes 221192 | tf_op jit(solution)/shard_map/ppermute | solution.py:20
  16.1 108.8 %collective-permute-start.6 = (bf16[3,3,512,256]{3,2,1,0:T(8,128)(2,1)}, bf16[3,3,512,256]{3,2,1,0:T(8,128)(2,1)}, u32[]{:S(2)}, u32[]{:S(2)}) collective-permute-start(bf16[3,3,512,256]{3,2,1,0:T(8,128)(2,1)} %param.26), channel_id=1, source_target_pairs={{0,8},{8,0},{1,9},{9,1},{2,10},{10,2},{3,11},{11,3},{4,12},{12,4},... | collective-permute-start | bytes 7077896 | tf_op jit(solution)/shard_map/ppermute | solution.py:20
  16.6 37.9 %collective-permute-start.8 = (bf16[3,3,256,128]{3,2,1,0:T(8,128)(2,1)}, bf16[3,3,256,128]{3,2,1,0:T(8,128)(2,1)}, u32[]{:S(2)}, u32[]{:S(2)}) collective-permute-start(bf16[3,3,256,128]{3,2,1,0:T(8,128)(2,1)} %param.28), channel_id=1, source_target_pairs={{0,8},{8,0},{1,9},{9,1},{2,10},{10,2},{3,11},{11,3},{4,12},{12,4},... | collective-permute-start | bytes 1769480 | tf_op jit(solution)/shard_map/ppermute | solution.py:20
  17.1 4.9 %copy-start.16 = (bf16[3,3,128,64]{2,3,1,0:T(8,128)(2,1)S(1)}, bf16[3,3,128,64]{2,3,1,0:T(8,128)(2,1)}, u32[]{:S(2)}) copy-start(bf16[3,3,128,64]{2,3,1,0:T(8,128)(2,1)} %param.30) | copy-start | bytes 442372
  22.0 21.1 %collective-permute-start.10 = (bf16[3,3,128,64]{2,3,1,0:T(8,128)(2,1)S(1)}, bf16[3,3,128,64]{2,3,1,0:T(8,128)(2,1)S(1)}, u32[]{:S(2)}, u32[]{:S(2)}) collective-permute-start(bf16[3,3,128,64]{2,3,1,0:T(8,128)(2,1)S(1)} %copy-done.16), channel_id=1, source_target_pairs={{0,8},{8,0},{1,9},{9,1},{2,10},{10,2},{3,11},{11,3},{4,12},{12,4},... | collective-permute-start | bytes 442376 | tf_op jit(solution)/shard_map/ppermute | solution.py:20
  48.6 31.9 %all-to-all-start.1 = ((bf16[2,64,8,512]{3,1,0,2:T(8,128)(2,1)}), bf16[2,64,8,512]{3,1,0,2:T(8,128)(2,1)S(1)}, u32[]{:S(2)}, u32[]{:S(2)}) async-start(bf16[2,64,8,512]{3,1,0,2:T(8,128)(2,1)} %pad_maximum_fusion.2), calls=%async_computation.1 | async-start | bytes 2097152 | tf_op jit(solution)/shard_map/all_to_all | solution.py:283
  84.2 14.6 %copy-start.17 = (f32[1,64,64]{2,1,0:T(8,128)S(1)}, f32[1,64,64]{2,1,0:T(8,128)}, u32[]{:S(2)}) copy-start(f32[1,64,64]{2,1,0:T(8,128)} %param.18) | copy-start | bytes 49156
  86.1 11.0 %all-to-all-start.2 = ((f32[8,1,4096]{2,1,0:T(1,128)}), f32[8,1,4096]{2,1,0:T(1,128)S(1)}, u32[]{:S(2)}, u32[]{:S(2)}) async-start(f32[8,1,4096]{2,1,0:T(1,128)} %reshape.719), calls=%async_computation.2 | async-start | bytes 262144 | tf_op jit(solution)/shard_map/all_to_all | solution.py:349
  98.7 4.4 %copy-start.7 = (bf16[1,512,256]{2,1,0:T(8,128)(2,1)S(1)}, bf16[1,512,256]{2,1,0:T(8,128)(2,1)}, u32[]{:S(2)}) copy-start(bf16[1,512,256]{2,1,0:T(8,128)(2,1)} %get-tuple-element.81) | copy-start | bytes 786436
  98.7 4.4 %copy-start.8 = (bf16[1,512,256]{2,1,0:T(8,128)(2,1)S(1)}, bf16[1,512,256]{2,1,0:T(8,128)(2,1)}, u32[]{:S(2)}) copy-start(bf16[1,512,256]{2,1,0:T(8,128)(2,1)} %get-tuple-element.34) | copy-start | bytes 786436
  98.8 2.3 %collective-permute-start = (f32[64,64]{1,0:T(8,128)S(1)}, f32[64,64]{1,0:T(8,128)S(1)}, u32[]{:S(2)}, u32[]{:S(2)}) collective-permute-start(f32[64,64]{1,0:T(8,128)S(1)} %bitcast_add_fusion.2), channel_id=1, source_target_pairs={{0,8},{8,0},{1,9},{9,1},{2,10},{10,2},{3,11},{11,3},{4,12},{12,4},... | collective-permute-start | bytes 49160 | tf_op jit(solution)/shard_map/ppermute | solution.py:352
  101.1 18.6 %collective-permute-start.1 = (bf16[64,64]{1,0:T(8,128)(2,1)S(1)}, bf16[64,64]{1,0:T(8,128)(2,1)S(1)}, u32[]{:S(2)}, u32[]{:S(2)}) collective-permute-start(bf16[64,64]{1,0:T(8,128)(2,1)S(1)} %select_convert_fusion), channel_id=1, source_target_pairs={{0,2},{1,3},{2,4},{3,5},{4,6},{5,7},{8,10},{9,11},{10,12},{11,13},... | collective-permute-start | bytes 24584 | tf_op jit(solution)/shard_map/ppermute | solution.py:361
  103.1 21.8 %copy-start.4 = (bf16[3,3,512,256]{3,2,1,0:T(8,128)(2,1)S(1)}, bf16[3,3,512,256]{3,2,1,0:T(8,128)(2,1)}, u32[]{:S(2)}) copy-start(bf16[3,3,512,256]{3,2,1,0:T(8,128)(2,1)} %param.26) | copy-start | bytes 7077892
  113.6 6.1 %collective-permute-start.2 = (bf16[64,64]{1,0:T(8,128)(2,1)S(1)}, bf16[64,64]{1,0:T(8,128)(2,1)S(1)}, u32[]{:S(2)}, u32[]{:S(2)}) collective-permute-start(bf16[64,64]{1,0:T(8,128)(2,1)S(1)} %select_convert_fusion), channel_id=1, source_target_pairs={{0,1},{1,2},{2,3},{3,4},{4,5},{5,6},{6,7},{8,9},{9,10},{10,11},{11... | collective-permute-start | bytes 24584 | tf_op jit(solution)/shard_map/ppermute | solution.py:361
  116.8 5.6 %collective-permute-start.3 = (bf16[64,64]{1,0:T(8,128)(2,1)S(1)}, bf16[64,64]{1,0:T(8,128)(2,1)S(1)}, u32[]{:S(2)}, u32[]{:S(2)}) collective-permute-start(bf16[64,64]{1,0:T(8,128)(2,1)S(1)} %select_convert_fusion), channel_id=1, source_target_pairs={{1,0},{2,1},{3,2},{4,3},{5,4},{6,5},{7,6},{9,8},{10,9},{11,10},{12... | collective-permute-start | bytes 24584 | tf_op jit(solution)/shard_map/ppermute | solution.py:361
  118.1 6.8 %collective-permute-start.4 = (bf16[64,64]{1,0:T(8,128)(2,1)S(1)}, bf16[64,64]{1,0:T(8,128)(2,1)S(1)}, u32[]{:S(2)}, u32[]{:S(2)}) collective-permute-start(bf16[64,64]{1,0:T(8,128)(2,1)S(1)} %select_convert_fusion), channel_id=1, source_target_pairs={{2,0},{3,1},{4,2},{5,3},{6,4},{7,5},{10,8},{11,9},{12,10},{13,11},... | collective-permute-start | bytes 24584 | tf_op jit(solution)/shard_map/ppermute | solution.py:361
  129.5 41.3 %copy-start.1 = (bf16[1,3,64,4096]{3,2,1,0:T(8,128)(2,1)S(1)}, bf16[1,3,64,4096]{3,2,1,0:T(8,128)(2,1)}, u32[]{:S(2)}) copy-start(bf16[1,3,64,4096]{3,2,1,0:T(8,128)(2,1)} %param.20) | copy-start | bytes 4718596
  (11 other events, 37.4 us)
where the time goes:
time: 172 us; the launch traced here: 171 us
  other arithmetic  41.5 us (24%)
  Pallas kernels  38.4 us (22%)
  local copies, waits for them, and re-layouts  29.9 us (17%)
  waiting for transfers between devices  27.4 us (16%)
  starting transfers between devices  26.7 us (16%)
  matrix products  5.62 us (3%)
    pallas_call x1, Pallas kernels, decode(): pl.pallas_call(decode_kernel, out_shape=jax.ShapeDtypeStruct((8, rgb, 8 *...  38.4 us
    all_to_all x1, waiting for transfers between devices, spread_full(): lax.all_to_all(pair_rows, 'seq', split_axis=2, concat_axis=1, tiled=True)  17.3 us
    another operation x2, other arithmetic, lifted_weight(): return jnp.stack(cells)  13.2 us
    transpose x1, other arithmetic, token_weight(): return stack.transpose(2, 4, 3, 5, 6, 0, 1, 7).reshape(36 * chans, 4 * outs)  8.94 us
    ppermute x4, starting transfers between devices, body(): rows.append(lax.ppermute(low_final, 'seq', pairs))  7.95 us
    all_to_all x1, starting transfers between devices, spread_full(): lax.all_to_all(query_rows, 'seq', split_axis=2, concat_axis=1, tiled=True)  7.35 us
    reshape x1, local copies, waits for them, and re-layouts, token_weight(): return stack.transpose(2, 4, 3, 5, 6, 0, 1, 7).reshape(36 * chans, 4 * outs)  6.56 us
    all_to_all x1, starting transfers between devices, spread_full(): lax.all_to_all(pair_rows, 'seq', split_axis=2, concat_axis=1, tiled=True)  5.93 us
  transfers between devices with their start and end apart: 14, of which 4 were waited for; matrix products, arithmetic and copies ran while one was open for 40% of the time, Pallas kernels for 0%

commit v1 on v0

v1 whole, which is shorter than its diff:
```python
import functools
import math

import jax
import jax.numpy as jnp
from jax import lax
from jax.experimental import pallas as pl
from jax.experimental.pallas import tpu as pltpu
from jax.sharding import PartitionSpec as P

HEADS = 32
HSIZE = 128


step_size = -0.5
norm_eps = 1e-06


MESH = pl.DeviceIdType.MESH


def lift(weight, lifted):
    depth = weight.shape[1]
    chunk = 64

    @pl.loop(0, depth // chunk)
    def _(i):
        row = pl.multiple_of(i * chunk, chunk)
        w = [weight[t, pl.ds(row, chunk)].astype(jnp.float32) for t in range(9)]

        def pairs(x, y, z):
            return ((x, y + z), (x + y, z))

        by_row = [pairs(w[q], w[3 + q], w[6 + q]) for q in range(3)]
        for a in (0, 1):
            for p in (0, 1):
                cols = pairs(*(by_row[q][a][p] for q in range(3)))
                for b in (0, 1):
                    for q in (0, 1):
                        at = pl.multiple_of((2 * p + q) * depth + row, chunk)
                        lifted[2 * a + b, pl.ds(at, chunk)] = cols[b][q].astype(jnp.bfloat16)


def front_kernel(
    splits, heads_here, sections, devices,
    latent, cond, embed, table, picks, out_proj, up2, up3, w_in, w_first, w_second, w_third,
    handed, tokens, o_up2, o_up3, i_up2, i_up3, i_in, i_first, i_second, i_third,
    proj, got_q, got_kv, partial, parts, result, low_final, rows, got_result, l_up2, l_up3,
    send_q, recv_q, send_kv, recv_kv, own_sem, send_p, recv_p, send_w, recv_w, keep_sem,
    send_h, recv_h, send_r, recv_r,
):
    f32, bf16 = jnp.float32, jnp.bfloat16
    me = lax.axis_index("seq")
    section = lax.axis_index("section")
    groups = devices // splits
    count = latent.shape[0]
    half = count // splits
    width = got_q.shape[1]
    size = width // heads_here
    my_group = me // splits

    barrier = pltpu.get_barrier_semaphore()
    for t in range(sections):

        @pl.loop(0, devices)
        def _(d):
            @pl.when(jnp.logical_or(d != me, section != t))
            def _():
                pl.semaphore_signal(
                    barrier, inc=1, device_id={"section": t, "seq": d}, device_id_type=MESH
                )

    pl.semaphore_wait(barrier, sections * devices - 1)

    low = latent[...].astype(bf16)
    partner = {"section": lax.rem(section + 1, sections)}

    def weight_copy(src, dst, k):
        return pltpu.make_async_remote_copy(
            src_ref=src, dst_ref=dst, send_sem=send_w.at[k], recv_sem=recv_w.at[k],
            device_id=partner, device_id_type=MESH,
        )

    def q_copy(d, src):
        return pltpu.make_async_remote_copy(
            src_ref=proj.at[d // splits, 0, pl.ds(lax.rem(d, splits) * half, half)],
            dst_ref=got_q.at[pl.ds(src * half, half)],
            send_sem=send_q.at[d], recv_sem=recv_q.at[src],
            device_id={"seq": d}, device_id_type=MESH,
        )

    def kv_copy(d, src):
        return pltpu.make_async_remote_copy(
            src_ref=proj.at[d // splits, pl.ds(1, 2)],
            dst_ref=got_kv.at[:, pl.ds(src * count, count)],
            send_sem=send_kv.at[d], recv_sem=recv_kv.at[src],
            device_id={"seq": d}, device_id_type=MESH,
        )

    @pl.loop(0, groups)
    def _(k):
        g = lax.rem(my_group + 1 + k, groups)
        lanes = pl.ds(pl.multiple_of(g * width, 128), width)
        audio = jnp.dot(picks[...], table[:, lanes], preferred_element_type=f32)
        for c in range(3):
            value = jnp.dot(low, embed[c, :, lanes], preferred_element_type=f32)
            value = value + cond[c, :, lanes].astype(f32)
            if c != 1:
                value = value + audio
            proj[g, c] = value.astype(bf16)

        @pl.loop(0, splits)
        def _(r):
            d = g * splits + r

            @pl.when(d != me)
            def _():
                q_copy(d, me).start()
                kv_copy(d, me).start()

    own_q = pltpu.make_async_copy(
        proj.at[my_group, 0, pl.ds(lax.rem(me, splits) * half, half)],
        got_q.at[pl.ds(me * half, half)], own_sem.at[0],
    )
    own_kv = pltpu.make_async_copy(
        proj.at[my_group, pl.ds(1, 2)], got_kv.at[:, pl.ds(me * count, count)], own_sem.at[1]
    )
    own_q.start()
    own_kv.start()
    plain = [
        weight_copy(w_in, i_in, 0), weight_copy(w_first, i_first, 1),
        weight_copy(w_second, i_second, 2), weight_copy(w_third, i_third, 3),
    ]
    for copy in plain:
        copy.start()
    lift(up2, l_up2)
    lift(up3, l_up3)
    made = [weight_copy(l_up2, i_up2, 4), weight_copy(l_up3, i_up3, 5)]
    kept = [
        pltpu.make_async_copy(l_up2, o_up2, keep_sem.at[0]),
        pltpu.make_async_copy(l_up3, o_up3, keep_sem.at[1]),
    ]
    for copy in made + kept:
        copy.start()

    own_q.wait()
    own_kv.wait()

    @pl.loop(0, devices)
    def _(d):
        @pl.when(d != me)
        def _():
            q_copy(d, d).wait_recv()
            kv_copy(d, d).wait_recv()

    query_count = got_q.shape[0]
    block = min(256, query_count)
    scale = 1.0 / math.sqrt(size)

    @pl.loop(0, query_count // block)
    def _(i):
        at = pl.ds(pl.multiple_of(i * block, block), block)
        total = jnp.zeros((block, out_proj.shape[1]), f32)
        for h in range(heads_here):
            lanes = slice(h * size, (h + 1) * size)
            scores = lax.dot_general(
                got_q[at, lanes], got_kv[0, :, lanes], (((1,), (1,)), ((), ())),
                preferred_element_type=f32,
            ) * scale
            row_max = jnp.max(scores, axis=1, keepdims=True)
            weights = jnp.exp(scores - row_max)
            denominator = jnp.sum(weights, axis=1, keepdims=True)
            attended = jnp.dot(
                weights.astype(bf16), got_kv[1, :, lanes], preferred_element_type=f32
            ) / denominator
            rows_of = pl.ds(pl.multiple_of(my_group * width + h * size, size), size)
            total = total + jnp.dot(
                attended.astype(bf16), out_proj[rows_of], preferred_element_type=f32
            )
        partial[at] = total

    def part_copy(d, src):
        return pltpu.make_async_remote_copy(
            src_ref=partial.at[pl.ds(d * half, half)],
            dst_ref=parts.at[src],
            send_sem=send_p.at[d], recv_sem=recv_p.at[src],
            device_id={"seq": d}, device_id_type=MESH,
        )

    @pl.loop(0, devices)
    def _(k):
        d = lax.rem(me + k, devices)

        @pl.when(d != me)
        def _():
            part_copy(d, me).start()

    @pl.loop(0, devices)
    def _(d):
        @pl.when(d != me)
        def _():
            part_copy(d, d).wait_recv()

    for r in range(splits):
        at = slice(r * half, (r + 1) * half)

        def add(g, total):
            d = g * splits + r
            own = partial[pl.ds(pl.multiple_of(me * half, half), half)]
            return total + jnp.where(d == me, own, parts[d])

        velocity = lax.fori_loop(0, groups, add, jnp.zeros((half, latent.shape[1]), f32))
        result[at] = latent[at] + step_size * velocity
    low_final[...] = result[...].astype(bf16)

    last = section == sections - 1
    given = pltpu.make_async_remote_copy(
        src_ref=result, dst_ref=got_result, send_sem=send_r, recv_sem=recv_r,
        device_id=partner, device_id_type=MESH,
    )
    given.start()

    def row_copy(by, t, to):
        slot = {2: 0, 1: 1, -1: 2, -2: 3}[by]
        return pltpu.make_async_remote_copy(
            src_ref=low_final, dst_ref=rows.at[slot],
            send_sem=send_h.at[slot, t], recv_sem=recv_h.at[slot],
            device_id={"section": t, "seq": lax.rem(to + devices, devices)}, device_id_type=MESH,
        )

    for by in (2, -2, 1, -1):
        for t in range(sections):
            inside = jnp.logical_and(me + by >= 0, me + by < devices)

            @pl.when(jnp.logical_and(last, inside))
            def _():
                row_copy(by, t, me + by).start()

    given.wait_recv()
    handed[...] = got_result[...]

    @pl.when(last)
    def _():
        tokens[2] = low_final[...]

    @pl.when(jnp.logical_not(last))
    def _():
        tokens[2] = got_result[...].astype(bf16)

    for by, slot, at in ((2, 0, 0), (1, 1, 1), (-1, 2, 3), (-2, 3, 4)):
        inside = jnp.logical_and(me - by >= 0, me - by < devices)

        @pl.when(inside)
        def _():
            row_copy(by, 0, me - by).wait_recv()
            tokens[at] = rows[slot]

        @pl.when(jnp.logical_not(inside))
        def _():
            tokens[at] = jnp.zeros(tokens.shape[1:], bf16)

    for by in (2, -2, 1, -1):
        for t in range(sections):
            inside = jnp.logical_and(me + by >= 0, me + by < devices)

            @pl.when(jnp.logical_and(last, inside))
            def _():
                row_copy(by, t, me + by).wait_send()

    given.wait_send()

    @pl.loop(0, devices)
    def _(d):
        @pl.when(d != me)
        def _():
            q_copy(d, me).wait_send()
            kv_copy(d, me).wait_send()
            part_copy(d, me).wait_send()

    for copy in kept + plain + made:
        copy.wait()


def front(latent, cond, embed, table, picks, out_proj, halves, splits, groups, width):
    w_in, w_first, up2, w_second, up3, w_third = halves
    devices, sections = lax.axis_size("seq"), lax.axis_size("section")
    f32, bf16 = jnp.float32, jnp.bfloat16
    count, patch = latent.shape
    half = count // splits
    heads_here = width // HSIZE
    vmem, hbm = pl.BlockSpec(memory_space=pltpu.VMEM), pl.BlockSpec(memory_space=pl.ANY)
    like = lambda a: jax.ShapeDtypeStruct(a.shape, a.dtype)
    lifted = lambda w: jax.ShapeDtypeStruct((4, 4 * w.shape[1], w.shape[2]), bf16)
    dma = pltpu.SemaphoreType.DMA
    l2, l3 = lifted(up2), lifted(up3)
    return pl.pallas_call(
        functools.partial(front_kernel, splits, heads_here, sections, devices),
        out_shape=(
            like(latent), jax.ShapeDtypeStruct((5, count, patch), bf16),
            l2, l3, l2, l3, like(w_in), like(w_first), like(w_second), like(w_third),
        ),
        in_specs=[vmem] * 8 + [hbm] * 4,
        out_specs=(vmem, vmem) + (hbm,) * 8,
        scratch_shapes=[
            pltpu.VMEM((groups, 3, count, width), bf16),
            pltpu.VMEM((devices * half, width), bf16),
            pltpu.VMEM((2, devices * count, width), bf16),
            pltpu.VMEM((devices * half, patch), f32),
            pltpu.VMEM((devices, half, patch), f32),
            pltpu.VMEM((count, patch), f32),
            pltpu.VMEM((count, patch), bf16),
            pltpu.VMEM((4, count, patch), bf16),
            pltpu.VMEM((count, patch), f32),
            pltpu.VMEM(l2.shape, bf16),
            pltpu.VMEM(l3.shape, bf16),
            dma((devices,)), dma((devices,)), dma((devices,)), dma((devices,)), dma((2,)),
            dma((devices,)), dma((devices,)), dma((6,)), dma((6,)), dma((2,)),
            dma((4, sections)), dma((4,)), dma, dma,
        ],
        compiler_params=pltpu.CompilerParams(
            collective_id=0, has_side_effects=True, vmem_limit_bytes=48 * 1024 * 1024
        ),
    )(latent, cond, embed, table, picks, out_proj, up2, up3, w_in, w_first, w_second, w_third)


def decode_kernel(
    keep, tokens, w_color, g1, g2, g3, g4,
    h_in, h_first, h_up2, h_second, h_up3, h_third,
    t_in, t_first, t_up2, t_second, t_up3, t_third,
    out, a1, p1, x1, a2, p2, x2, a3, p3, p4,
    w_in, w_first, w_up2, w_second, b_up3, b_third, w_up3, w_third, sems,
):
    section = lax.axis_index("section")
    loads = []
    for own, source in ((0, (h_in, h_first, h_up2, h_second, h_up3, h_third)),
                        (1, (t_in, t_first, t_up2, t_second, t_up3, t_third))):
        place = lax.rem(section + own, 2)
        for k, (src, dst) in enumerate(
            zip(source, (w_in, w_first, w_up2, w_second, b_up3, b_third))
        ):
            if k < 4:
                lanes = src.shape[-1]
                at = pl.ds(pl.multiple_of(place * lanes, 128), lanes)
                view = dst.at[:, :, at] if len(dst.shape) == 3 else dst.at[:, at]
            else:
                view = dst.at[place]
            copy = pltpu.make_async_copy(src, view, sems.at[own, k])
            copy.start()
            loads.append((k, copy))

    def ready(index):
        for k, copy in loads:
            if k == index:
                copy.wait()

    cols = tokens.shape[1]
    f32, bf16 = jnp.float32, jnp.bfloat16
    k_a, k_b, k_c, k_d = keep[0], keep[1], keep[2], keep[3]

    def moved(value, by):
        position = lax.broadcasted_iota(jnp.int32, value.shape, 0)
        if by > 0:
            return jnp.where(position > 0, pltpu.roll(value, 1, 0), 0.0)
        return jnp.where(position < cols - 1, pltpu.roll(value, cols - 1, 0), 0.0)

    def put(buf, index, value):
        phases = value.shape[0]
        buf[index, 1 : phases + 1] = value.astype(bf16)
        buf[index, 0] = moved(value[phases - 1], 1).astype(bf16)
        buf[index, phases + 1] = moved(value[0], -1).astype(bf16)

    def act(value, gain):
        square = jnp.mean(value * value, axis=-1, keepdims=True)
        scaled = value * lax.rsqrt(square + norm_eps) * gain[...]
        return jax.nn.silu(scaled)

    def fill(source, buf, count, where_to, masked, gain=None, offset=0):
        @pl.loop(0, count)
        def _(i):
            value = source[i + offset].astype(f32)
            put(buf, where_to(i), value if gain is None else act(value, gain))

        for target, origin, factor in masked:
            if origin is None:
                buf[target] = jnp.zeros(buf.shape[1:], bf16)
            else:
                buf[target] = (buf[origin].astype(f32) * factor).astype(bf16)

    def spots(*bounds):
        def start(o):
            index = o
            for bound in bounds:
                index = index + 2 * (o >= bound).astype(jnp.int32)
            return index

        return start

    def window(buf, start, rows, taps_r, taps_c, phases):
        parts = []
        for p in taps_r:
            for q in taps_c:
                block = buf[pl.ds(start + p, rows), q : q + phases]
                parts.append(block.reshape(rows * phases * cols, block.shape[-1]))
        return jnp.concatenate(parts, axis=1)

    def dot(x, w):
        return jnp.dot(x, w, preferred_element_type=f32)

    full = tokens[...].astype(f32)
    count = full.shape[0]
    zero = jnp.zeros((1,) + full.shape[1:], f32)
    ks = (k_a, k_b, k_c, k_d)
    above = jnp.concatenate([zero] + [full[i : i + 1] * ks[i] for i in range(count - 1)])
    below = jnp.concatenate([full[i + 1 : i + 2] * ks[i] for i in range(count - 1)] + [zero])
    pieces = []
    for rows in (above, full, below):
        left = jnp.stack([moved(rows[i], 1) for i in range(count)])
        right = jnp.stack([moved(rows[i], -1) for i in range(count)])
        pieces += [left, rows, right]
    x = jnp.concatenate(pieces, axis=2).astype(bf16).reshape(count * cols, -1)
    cell = tokens.shape[2]
    chans = cell // 4
    column = lax.broadcasted_iota(jnp.int32, (9 * cell, 9 * chans), 1)
    line = lax.broadcasted_iota(jnp.int32, (9 * cell, 9 * chans), 0)
    tap = column // chans
    tap_r = (tap >= 3).astype(jnp.int32) + (tap >= 6).astype(jnp.int32)
    tap_c = tap - 3 * tap_r
    ready(0)
    for a in (0, 1):
        for b in (0, 1):
            u, v = tap_r + (a + 1), tap_c + (b + 1)
            wanted = ((u >> 1) * 3 + (v >> 1)) * cell + (2 * (u & 1) + (v & 1)) * chans
            pick = (line == wanted + column - tap * chans).astype(f32).astype(bf16)
            y = dot(dot(x, pick).astype(bf16), w_in[...]).astype(bf16)
            for i in range(count):
                a1[2 * i + a, b] = y[i * cols : (i + 1) * cols]

    def spot1(i):
        return i + 1 + 2 * (i >= 2).astype(jnp.int32) + 2 * (i >= 4).astype(jnp.int32)

    inner = ((3, 5, k_b), (4, 2, k_b), (7, 9, k_c), (8, 6, k_c))
    fill(a1, p1, 6, spot1, inner, g1, 2)
    for target, origin, factor in ((0, 1, k_a), (11, 8, k_d)):
        put(p1, target, act(a1[origin].astype(f32), g1) * factor)
    ready(1)

    @pl.loop(0, 3)
    def _(i):
        y = dot(window(p1, 4 * i, 2, (0, 1, 2), (0, 1, 2), 2), w_first[...])
        base = a1[pl.ds(2 * i + 2, 2)]
        a1[pl.ds(2 * i + 2, 2)] = (base.astype(f32) + y.reshape(base.shape)).astype(bf16)

    fill(a1, x1, 6, spot1, inner + ((0, None, 0), (11, None, 0)), None, 2)

    ready(2)
    @pl.loop(0, 3)
    def _(i):
        for a in (0, 1):
            for b in (0, 1):
                y = dot(window(x1, 4 * i, 2, (a, a + 1), (b, b + 1), 2), w_up2[2 * a + b])
                y = y.astype(bf16).reshape(2, 2, cols, -1)
                for r in (0, 1):
                    for f in (0, 1):
                        a2[4 * i + 2 * r + a, 2 * f + b] = y[r, f]

    fill(
        a2, p2, 10,
        lambda i: i + 2 * (i >= 3).astype(jnp.int32) + 2 * (i >= 7).astype(jnp.int32),
        ((3, 5, k_b), (4, 2, k_b), (9, 11, k_c), (10, 8, k_c)), g2, 1,
    )
    start2 = spots(2, 6)
    ready(3)

    @pl.loop(0, 8)
    def _(o):
        y = dot(window(p2, start2(o), 1, (0, 1, 2), (0, 1, 2), 4), w_second[...])
        base = a2[o + 2]
        a2[o + 2] = (base.astype(f32) + y.reshape(base.shape)).astype(bf16)

    fill(
        a2, x2, 8,
        lambda i: i + 2 * (i >= 2).astype(jnp.int32) + 2 * (i >= 6).astype(jnp.int32),
        ((2, 4, k_b), (3, 1, k_b), (8, 10, k_c), (9, 7, k_c)), None, 2,
    )
    start3 = spots(1, 5)

    ready(4)
    ready(5)
    w_up3[...] = jnp.concatenate([b_up3[0], b_up3[1]], axis=2)
    w_third[...] = jnp.concatenate([b_third[0], b_third[1]], axis=1)

    @pl.loop(0, 6)
    def _(o):
        for a in (0, 1):
            for b in (0, 1):
                y = dot(window(x2, start3(o), 1, (a, a + 1), (b, b + 1), 4), w_up3[2 * a + b])
                y = y.astype(bf16).reshape(4, cols, -1)
                for f in range(4):
                    a3[2 * o + a, 2 * f + b] = y[f]

    fill(
        a3, p3, 12,
        lambda i: i + 2 * (i >= 2).astype(jnp.int32) + 2 * (i >= 10).astype(jnp.int32),
        ((2, 4, k_b), (3, 1, k_b), (12, 14, k_c), (13, 11, k_c)), g3,
    )
    start4 = spots(1, 9)

    @pl.loop(0, 10)
    def _(o):
        y = dot(window(p3, start4(o), 1, (0, 1, 2), (0, 1, 2), 8), w_third[...])
        base = a3[o + 1]
        value = (base.astype(f32) + y.reshape(base.shape)).astype(bf16).astype(f32)
        put(p4, o, act(value, g4))

    for target, factor in ((0, k_b), (9, k_c)):
        p4[target] = (p4[target].astype(f32) * factor).astype(bf16)

    @pl.loop(0, 8)
    def _(o):
        patch = window(p4, o, 1, (0, 1, 2), (0, 1, 2), 8)
        colors = lax.dot_general(
            w_color[...], patch, (((1,), (1,)), ((), ())), preferred_element_type=f32
        )
        for k in range(out.shape[0]):
            out[k, pl.ds(o, 1)] = colors[k : k + 1]


def decode(tokens, keep, color, gains, own, other, rgb):
    count, cols = tokens.shape[:2]
    c1, c2, c3 = (2 * own[k].shape[-1] for k in (1, 3, 5))
    bf16 = jnp.bfloat16
    vmem, hbm = pl.BlockSpec(memory_space=pltpu.VMEM), pl.BlockSpec(memory_space=pl.ANY)
    wide = lambda w: pltpu.VMEM(w.shape[:-1] + (2 * w.shape[-1],), bf16)
    return pl.pallas_call(
        decode_kernel,
        out_shape=jax.ShapeDtypeStruct((rgb, 8, 8 * cols), jnp.float32),
        in_specs=[pl.BlockSpec(memory_space=pltpu.SMEM)] + [vmem] * 6 + [hbm] * 12,
        out_specs=vmem,
        scratch_shapes=[
            pltpu.VMEM((2 * count, 2, cols, c1), bf16),
            pltpu.VMEM((12, 4, cols, c1), bf16),
            pltpu.VMEM((12, 4, cols, c1), bf16),
            pltpu.VMEM((12, 4, cols, c2), bf16),
            pltpu.VMEM((14, 6, cols, c2), bf16),
            pltpu.VMEM((12, 6, cols, c2), bf16),
            pltpu.VMEM((12, 8, cols, c3), bf16),
            pltpu.VMEM((16, 10, cols, c3), bf16),
            pltpu.VMEM((10, 10, cols, c3), bf16),
            wide(own[0]), wide(own[1]), wide(own[2]), wide(own[3]),
            pltpu.VMEM((2,) + own[4].shape, bf16), pltpu.VMEM((2,) + own[5].shape, bf16),
            wide(own[4]), wide(own[5]),
            pltpu.SemaphoreType.DMA((2, 6)),
        ],
        compiler_params=pltpu.CompilerParams(vmem_limit_bytes=56 * 1024 * 1024),
    )(keep, tokens, color, *gains, *own, *other)


def body(
    latents,
    cond,
    embed,
    audio_table,
    audio_map,
    out_proj,
    tile_start,
    conv_input,
    conv_first,
    conv_second_up,
    conv_second,
    conv_third_up,
    conv_third,
    conv_color,
    gain_first,
    gain_second,
    gain_third,
    gain_color,
):
    latent = latents[0]
    tokens_here = latent.shape[0]
    frame_count = audio_table.shape[1]
    frames = jnp.repeat(audio_map, tokens_here // audio_map.shape[0])
    picks = (frames[:, None] == lax.broadcasted_iota(jnp.int32, (1, frame_count), 1)).astype(
        jnp.bfloat16
    )
    devices = lax.axis_size("seq")
    splits = max(devices // HEADS, 1)
    per_device = max(HEADS // devices, 1)
    groups = HEADS // per_device
    flat = lambda w: w.reshape(-1, w.shape[-1])
    taps = lambda w: w.reshape(9, *w.shape[2:])
    halves = (
        flat(conv_input), flat(conv_first), taps(conv_second_up),
        flat(conv_second), taps(conv_third_up), flat(conv_third),
    )
    handed, tokens, o_up2, o_up3, i_up2, i_up3, i_in, i_first, i_second, i_third = front(
        latent, cond[0], embed[0], audio_table[0], picks, out_proj[0], halves, splits, groups,
        per_device * HSIZE,
    )
    position = lax.axis_index("seq")
    block = position + jnp.arange(-2, 2)
    following = jnp.clip(block + 1, 0, devices - 1)
    inside = jnp.logical_and(block >= 0, block + 1 < devices)
    keep = jnp.where(jnp.logical_and(inside, tile_start[following] == 0), 1.0, 0.0)
    color = jnp.pad(flat(conv_color).T, ((0, 8 - conv_color.shape[3]), (0, 0)))
    gains = tuple(g[None] for g in (gain_first, gain_second, gain_third, gain_color))
    own = (halves[0], halves[1], o_up2, halves[3], o_up3, halves[5])
    other = (i_in, i_first, i_up2, i_second, i_up3, i_third)
    rgb = conv_color.shape[3]
    colors = decode(tokens, keep.astype(jnp.float32), color, gains, own, other, rgb)
    image = colors.reshape(rgb, 8, 8, -1).transpose(0, 1, 3, 2).reshape(rgb, 8, -1)
    return (handed[None], image)


def solution(mesh):
    in_specs = (
        P("section", ("replica", "seq"), None),
        P("section", None, ("replica", "seq"), None),
        P("section", None, None, None),
        P("section", "replica", None),
        P(("replica", "seq")),
        P("section", None, None),
        P("replica"),
        P(None, None, None, "section"),
        P(None, None, None, "section"),
        P(None, None, None, "section"),
        P(None, None, None, "section"),
        P(None, None, None, "section"),
        P(None, None, None, "section"),
        P(),
        P(),
        P(),
        P(),
        P(),
    )
    out_specs = (P("section", ("replica", "seq"), None), P(None, ("replica", "seq"), None))
    return jax.shard_map(body, mesh=mesh, in_specs=in_specs, out_specs=out_specs, check_vma=False)
```

time: 172 us -> 111 us (0.65)
  Pallas kernels: 38.4 us -> 96.5 us
  other arithmetic: 41.5 us -> 0.63 us
  waiting for transfers between devices: 27.4 us -> 0 us
  starting transfers between devices: 26.7 us -> 0 us
  local copies, waits for them, and re-layouts: 29.9 us -> 12.3 us
  matrix products: 5.62 us -> 0 us
    pallas_call x1 -> x2, Pallas kernels: 38.4 us -> 96.5 us  [the longest x1 58.1 us: front(): pl.pallas_call(functools.partial(front_kernel, splits, heads_here, sectio...]
    all_to_all x3 -> x0, waiting for transfers between devices: 22.2 us -> none  [the longest x1 17.3 us: spread_full(): lax.all_to_all(pair_rows, 'seq', split_axis=2, concat_axis=1, tiled=True)]
    all_to_all x3 -> x0, starting transfers between devices: 16.9 us -> none  [the longest x1 7.35 us: spread_full(): lax.all_to_all(query_rows, 'seq', split_axis=2, concat_axis=1, tiled=True)]
    another operation x5 -> x0, other arithmetic: 16.3 us -> none  [the longest x2 13.2 us: lifted_weight(): return jnp.stack(cells)]
    ppermute x11 -> x0, starting transfers between devices: 9.73 us -> none  [the longest x4 7.95 us: body(): rows.append(lax.ppermute(low_final, 'seq', pairs))]
    transpose x1 -> x0, other arithmetic: 8.94 us -> none  [token_weight(): return stack.transpose(2, 4, 3, 5, 6, 0, 1, 7).reshape(36 * chans, 4 * outs)]
    another operation x10 -> x0, local copies, waits for them, and re-layouts: 6.94 us -> none  [the longest x4 4.7 us: token_weight(): stack = jnp.stack([jnp.stack(row) for row in cells])]
    concatenate x6 -> x0, other arithmetic: 6.03 us -> none  [the longest x4 3.81 us: full_weight(): jnp.concatenate([jnp.where(first, half, other), jnp.where(first, other, h...]
  transfers between devices with their start and end apart: 14 -> 0, of which waited for: 4 -> 0; matrix products, arithmetic and copies ran while one was open for 40% -> 0% of each run, Pallas kernels for 0% -> 0%
where the time goes in v1:
time: 111 us; the launch traced here: 110 us
  Pallas kernels  96.5 us (87%)
  local copies, waits for them, and re-layouts  12.3 us (11%)
    pallas_call x1, Pallas kernels, front(): pl.pallas_call(functools.partial(front_kernel, splits, heads_here, sectio...  58.1 us
    pallas_call x1, Pallas kernels, decode(): pl.pallas_call(decode_kernel, out_shape=jax.ShapeDtypeStruct((rgb, 8, 8 *...  38.4 us
    unnamed x34, local copies, waits for them, and re-layouts  8.71 us

profile of v1, /device:TPU:0, one launch (start us, length us, event | category | flops | bytes accessed | tf_op | source)
XLA Modules:
  0.0 110.3 jit_solution(10365745780794443461)
XLA Ops:
  0.6 0.0 copy-start
  0.6 0.0 copy-start.7
  0.7 1.2 %copy.27 = bf16[3,3,128,64]{3,2,1,0:T(8,128)(2,1)S(1)} copy(bf16[3,3,128,64]{2,3,1,0:T(8,128)(2,1)} %param.30) | data formatting | bytes 294912 | tf_op args[12]
  1.9 1.6 %copy.25 = bf16[1,4096,64]{2,1,0:T(8,128)(2,1)S(1)} copy(bf16[1,4096,64]{1,2,0:T(8,128)(2,1)} %param.23) | data formatting | bytes 1048576 | tf_op args[5]
  3.6 0.3 copy.26
  3.9 0.1 broadcast_in_dim.27
  4.0 0.1 eq.18
  4.1 0.1 fusion.picks
  4.2 0.0 copy-start.13
  4.2 58.1 %shard_map.185 = (f32[64,64]{1,0:T(8,128)S(1)}, bf16[5,64,64]{2,1,0:T(8,128)(2,1)S(1)}, bf16[4,2048,128]{2,1,0:T(8,128)(2,1)}, bf16[4,1024,64]{2,1,0:T(8,128)(2,...) custom-call(f32[64,64]{1,0:T(8,128)S(1)} %bitcast.33, ...), custom_call_target="tpu_custom_call" | custom-call | tf_op jit(solution)/shard_map/pallas_call | solution.py:296
  62.4 1.0 copy-done.3
  63.3 1.1 copy-done.4
  64.4 0.9 copy-done.5
  65.3 0.7 copy-done.6
  66.0 0.6 copy-done.9
  66.6 0.6 copy-done.10
  67.3 0.6 gather_fusion
  67.9 0.5 and_select_fusion.keep
  68.5 0.6 pad.4.w_color
  69.1 38.4 %shard_map.186 = f32[3,8,512]{2,1,0:T(8,128)} custom-call(f32[4]{0:T(128)} %and_select_fusion.keep, bf16[5,64,64]{2,1,0:T(8,128)(2,1)} %copy-done.9, bf16[8,1152]{1,0:T(8,128)(2,1)} %pad.4.w_color, f32[1,512]{1,0:T(1,128)} %bitcast.42, f32[1,256]{1,0:T(1,128)} %bitcast.43, f32[1,128]{1,0:T(1,128)} %bitcast.44, f32[1,128]{1,0:T(1,128)} %bitcast.45, ...), custom_call_target="tpu_custom_call" | custom-call | tf_op jit(solution)/shard_map/pallas_call | solution.py:534
  107.5 0.9 reshape.64
  108.4 0.3 copy.29
  108.6 1.0 reshape.65
  109.7 0.6 copy.31
  (23 shorter events, 0.1 us)
Async XLA Ops:
  0.6 66.6 %copy-start = (s32[8]{0:T(128)S(1)}, s32[8]{0:T(128)}, u32[]{:S(2)}) copy-start(s32[8]{0:T(128)} %param.24) | copy-start | bytes 100
  0.6 3.5 %copy-start.7 = (bf16[3,3,16,256]{3,2,1,0:T(8,128)(2,1)S(1)}, bf16[3,3,16,256]{3,2,1,0:T(8,128)(2,1)}, u32[]{:S(2)}) copy-start(bf16[3,3,16,256]{3,2,1,0:T(8,128)(2,1)} %param.25) | copy-start | bytes 221188
  0.7 3.5 %copy-start.2 = (bf16[3,3,256,128]{3,2,1,0:T(8,128)(2,1)S(1)}, bf16[3,3,256,128]{3,2,1,0:T(8,128)(2,1)}, u32[]{:S(2)}) copy-start(bf16[3,3,256,128]{3,2,1,0:T(8,128)(2,1)} %param.28) | copy-start | bytes 1769476
  0.7 2.9 %copy-start.12 = (bf16[3,3,256,64]{2,3,1,0:T(8,128)(2,1)S(1)}, bf16[3,3,256,64]{2,3,1,0:T(8,128)(2,1)}, u32[]{:S(2)}) copy-start(bf16[3,3,256,64]{2,3,1,0:T(8,128)(2,1)} %param.29) | copy-start | bytes 884740
  0.7 3.2 %copy-start.14 = (s32[4]{0:T(128)S(1)}, s32[4]{0:T(128)}, u32[]{:S(2)}) copy-start(s32[4]{0:T(128)} %param.22) | copy-start | bytes 52
  0.7 3.5 %copy-start.11 = (f32[1,64,64]{2,1,0:T(8,128)S(1)}, f32[1,64,64]{2,1,0:T(8,128)}, u32[]{:S(2)}) copy-start(f32[1,64,64]{2,1,0:T(8,128)} %param.18) | copy-start | bytes 49156
  0.7 3.5 %copy-start.8 = (bf16[1,32,4096]{2,1,0:T(8,128)(2,1)S(1)}, bf16[1,32,4096]{2,1,0:T(8,128)(2,1)}, u32[]{:S(2)}) copy-start(bf16[1,32,4096]{2,1,0:T(8,128)(2,1)} %param.21) | copy-start | bytes 786436
  1.9 60.4 %copy-start.1 = (bf16[3,3,128,64]{3,2,1,0:T(8,128)(2,1)}, bf16[3,3,128,64]{3,2,1,0:T(8,128)(2,1)S(1)}, u32[]{:S(2)}) copy-start(bf16[3,3,128,64]{3,2,1,0:T(8,128)(2,1)S(1)} %copy.27) | copy-start | bytes 442372
  4.2 64.3 %copy-start.13 = (bf16[3,3,128,3]{2,3,1,0:T(4,128)(2,1)S(1)}, bf16[3,3,128,3]{2,3,1,0:T(4,128)(2,1)}, u32[]{:S(2)}) copy-start(bf16[3,3,128,3]{2,3,1,0:T(4,128)(2,1)} %param.31) | copy-start | bytes 20740
  62.3 1.0 copy-start.3
  63.3 1.1 copy-start.4
  64.4 0.9 copy-start.5
  65.3 0.7 copy-start.6
  66.0 0.6 copy-start.9
  66.6 0.6 copy-start.10

commit v2 on v1

--- a/solution.py
+++ b/solution.py
@@ -529,7 +529,7 @@
     count, cols = tokens.shape[:2]
     c1, c2, c3 = (2 * own[k].shape[-1] for k in (1, 3, 5))
     bf16 = jnp.bfloat16
-    vmem, hbm = pl.BlockSpec(memory_space=pltpu.VMEM), pl.BlockSpec(memory_space=pl.ANY)
+    vmem, hbm = pl.BlockSpec(memory_space=pltpu.VMEM), pl.BlockSpec(memory_space=pltpu.HBM)
     wide = lambda w: pltpu.VMEM(w.shape[:-1] + (2 * w.shape[-1],), bf16)
     return pl.pallas_call(
         decode_kernel,

time: 111 us -> 111 us (level)
  no operation moved by 1% of the time
where the time goes in v2:
time: 111 us; the launch traced here: 110 us
  Pallas kernels  96.5 us (87%)
  local copies, waits for them, and re-layouts  12.3 us (11%)
    pallas_call x1, Pallas kernels, front(): pl.pallas_call(functools.partial(front_kernel, splits, heads_here, sectio...  58.1 us
    pallas_call x1, Pallas kernels, decode(): pl.pallas_call(decode_kernel, out_shape=jax.ShapeDtypeStruct((rgb, 8, 8 *...  38.4 us
    unnamed x34, local copies, waits for them, and re-layouts  8.71 us

profile of v2, /device:TPU:0, one launch (start us, length us, event | category | flops | bytes accessed | tf_op | source)
XLA Modules:
  0.0 110.3 jit_solution(10365745780794443461)
XLA Ops:
  0.6 0.0 copy-start
  0.6 0.0 copy-start.7
  0.7 1.2 %copy.27 = bf16[3,3,128,64]{3,2,1,0:T(8,128)(2,1)S(1)} copy(bf16[3,3,128,64]{2,3,1,0:T(8,128)(2,1)} %param.30) | data formatting | bytes 294912 | tf_op args[12]
  1.9 1.6 %copy.25 = bf16[1,4096,64]{2,1,0:T(8,128)(2,1)S(1)} copy(bf16[1,4096,64]{1,2,0:T(8,128)(2,1)} %param.23) | data formatting | bytes 1048576 | tf_op args[5]
  3.6 0.3 copy.26
  3.9 0.1 broadcast_in_dim.27
  4.0 0.1 eq.18
  4.1 0.1 fusion.picks
  4.2 0.0 copy-start.13
  4.2 58.1 %shard_map.185 = (f32[64,64]{1,0:T(8,128)S(1)}, bf16[5,64,64]{2,1,0:T(8,128)(2,1)S(1)}, bf16[4,2048,128]{2,1,0:T(8,128)(2,1)}, bf16[4,1024,64]{2,1,0:T(8,128)(2,...) custom-call(f32[64,64]{1,0:T(8,128)S(1)} %bitcast.33, ...), custom_call_target="tpu_custom_call" | custom-call | tf_op jit(solution)/shard_map/pallas_call | solution.py:296
  62.4 1.0 copy-done.3
  63.3 1.1 copy-done.4
  64.4 0.9 copy-done.5
  65.3 0.7 copy-done.6
  66.0 0.6 copy-done.9
  66.6 0.6 copy-done.10
  67.3 0.6 gather_fusion
  67.9 0.5 and_select_fusion.keep
  68.5 0.6 pad.4.w_color
  69.1 38.4 %shard_map.186 = f32[3,8,512]{2,1,0:T(8,128)} custom-call(f32[4]{0:T(128)} %and_select_fusion.keep, bf16[5,64,64]{2,1,0:T(8,128)(2,1)} %copy-done.9, bf16[8,1152]{1,0:T(8,128)(2,1)} %pad.4.w_color, f32[1,512]{1,0:T(1,128)} %bitcast.42, f32[1,256]{1,0:T(1,128)} %bitcast.43, f32[1,128]{1,0:T(1,128)} %bitcast.44, f32[1,128]{1,0:T(1,128)} %bitcast.45, ...), custom_call_target="tpu_custom_call" | custom-call | tf_op jit(solution)/shard_map/pallas_call | solution.py:534
  107.5 0.9 reshape.64
  108.4 0.3 copy.29
  108.6 1.0 reshape.65
  109.7 0.6 copy.31
  (23 shorter events, 0.1 us)
Async XLA Ops:
  0.6 66.6 %copy-start = (s32[8]{0:T(128)S(1)}, s32[8]{0:T(128)}, u32[]{:S(2)}) copy-start(s32[8]{0:T(128)} %param.24) | copy-start | bytes 100
  0.6 3.5 %copy-start.7 = (bf16[3,3,16,256]{3,2,1,0:T(8,128)(2,1)S(1)}, bf16[3,3,16,256]{3,2,1,0:T(8,128)(2,1)}, u32[]{:S(2)}) copy-start(bf16[3,3,16,256]{3,2,1,0:T(8,128)(2,1)} %param.25) | copy-start | bytes 221188
  0.7 3.5 %copy-start.2 = (bf16[3,3,256,128]{3,2,1,0:T(8,128)(2,1)S(1)}, bf16[3,3,256,128]{3,2,1,0:T(8,128)(2,1)}, u32[]{:S(2)}) copy-start(bf16[3,3,256,128]{3,2,1,0:T(8,128)(2,1)} %param.28) | copy-start | bytes 1769476
  0.7 2.9 %copy-start.12 = (bf16[3,3,256,64]{2,3,1,0:T(8,128)(2,1)S(1)}, bf16[3,3,256,64]{2,3,1,0:T(8,128)(2,1)}, u32[]{:S(2)}) copy-start(bf16[3,3,256,64]{2,3,1,0:T(8,128)(2,1)} %param.29) | copy-start | bytes 884740
  0.7 3.2 %copy-start.14 = (s32[4]{0:T(128)S(1)}, s32[4]{0:T(128)}, u32[]{:S(2)}) copy-start(s32[4]{0:T(128)} %param.22) | copy-start | bytes 52
  0.7 3.5 %copy-start.11 = (f32[1,64,64]{2,1,0:T(8,128)S(1)}, f32[1,64,64]{2,1,0:T(8,128)}, u32[]{:S(2)}) copy-start(f32[1,64,64]{2,1,0:T(8,128)} %param.18) | copy-start | bytes 49156
  0.7 3.5 %copy-start.8 = (bf16[1,32,4096]{2,1,0:T(8,128)(2,1)S(1)}, bf16[1,32,4096]{2,1,0:T(8,128)(2,1)}, u32[]{:S(2)}) copy-start(bf16[1,32,4096]{2,1,0:T(8,128)(2,1)} %param.21) | copy-start | bytes 786436
  1.9 60.4 %copy-start.1 = (bf16[3,3,128,64]{3,2,1,0:T(8,128)(2,1)}, bf16[3,3,128,64]{3,2,1,0:T(8,128)(2,1)S(1)}, u32[]{:S(2)}) copy-start(bf16[3,3,128,64]{3,2,1,0:T(8,128)(2,1)S(1)} %copy.27) | copy-start | bytes 442372
  4.2 64.3 %copy-start.13 = (bf16[3,3,128,3]{2,3,1,0:T(4,128)(2,1)S(1)}, bf16[3,3,128,3]{2,3,1,0:T(4,128)(2,1)}, u32[]{:S(2)}) copy-start(bf16[3,3,128,3]{2,3,1,0:T(4,128)(2,1)} %param.31) | copy-start | bytes 20740
  62.3 1.0 copy-start.3
  63.3 1.1 copy-start.4
  64.4 0.9 copy-start.5
  65.3 0.7 copy-start.6
  66.0 0.6 copy-start.9
  66.6 0.6 copy-start.10
